TPU v7x, 512 devices: a whole 4x4x16 slice. The times are simulated.
512 devices in a mesh: cube: 16 (over x, z_hi, core), tile: 32 (over y, z_lo).
Axes of the slice: x: 4, y: 4, z: 16 (z_hi: 2, z_lo: 8; z = z_hi * 8 + z_lo), core: 2. Of those that a mesh axis runs over, the one named last changes fastest.
Arguments:
- leaf_fronts: float32 [8, 4096, 1, 8192], P(None, 'cube', None, 'tile'), as said below
- middle_fronts: float32 [4, 4096, 1, 8192], P(None, 'cube', None, 'tile'), as said below
- root_front: float32 [2, 4096, 1, 8192], P(None, 'cube', None, 'tile'), as said below
- leaf_scatter: int32 [4, 32, 256], replicated, may hold values from 0 to 255, each once within a row
- middle_scatter: int32 [2, 32, 256], replicated, may hold values from 0 to 255, each once within a row
- leaf_orders: int32 [4], replicated, may hold values from 4096 to 8192, as said below
- middle_orders: int32 [2], replicated, may hold values from 4096 to 8192, as said below
Outputs:
- leaf_panel: bfloat16 [8, 16, 256, 256], P(None, 'cube', 'tile')
- middle_panel: bfloat16 [4, 16, 256, 256], P(None, 'cube', 'tile')
- root_panel: bfloat16 [2, 16, 256, 256], P(None, 'cube', 'tile')
- root_schur: bfloat16 [2, 4096, 1, 8192], P(None, 'cube', None, 'tile')
Inputs may be any that keep to these rules, and one draw needn't show every extreme that they name: `leaf_fronts`: each front is symmetric and positive definite. `middle_fronts`: each front is symmetric and positive definite. `root_front`: the front is symmetric and positive definite. `leaf_orders`: some front of the level has all 8192 rows live. `middle_orders`: some front of the level has all 8192 rows live.
All inputs are finite; a program needn't handle non-finite values.
Results may differ from a plain program's by a relative error of at most 0.0052.
Values may be sent and summed in bfloat16 or wider, within the bound.
A program may use at most 64 MiB of HBM per device.

v0:
```python
import jax
import jax.numpy as jnp
from jax import lax
from jax.sharding import Mesh
from jax.sharding import PartitionSpec as P

TILE = ("tile_0", "tile_1")


def partner_2(block, axis, apart):
    count = lax.axis_size(axis)
    route = []
    for low in range(count):
        high = low | 1 << apart
        if high != low and high < count:
            route += [(low, high), (high, low)]
    return lax.ppermute(block, axis, route)


def from_root(value, axes, root):
    value = jnp.where(lax.axis_index(axes) == root, value, jnp.zeros_like(value))
    for axis in axes:
        value = lax.psum(value, axis)
    return value


def bit_list(groups):
    levels = groups.bit_length() - 1
    return list(range(levels))


def spread_corner(payload, groups):
    for which_bit in bit_list(groups):
        payload = payload + partner_2(payload, "cube", which_bit)
    return payload


def spread_columns(payload, groups):
    for which_bit in bit_list(groups):
        payload = payload + partner_2(payload, "cube", which_bit)
    return payload


def solve_strip(strip_rows, corner, row_ids, pivot_tile):
    tile_width = strip_rows.shape[1]
    lower_factor = jnp.linalg.cholesky(corner)
    flat_strip = strip_rows.reshape(-1, tile_width)
    solved = jax.scipy.linalg.solve_triangular(lower_factor, flat_strip.T, lower=True).T
    solved = solved.reshape(strip_rows.shape)
    solved = jnp.where((row_ids == pivot_tile)[:, None, None], lower_factor[None], solved)
    return solved.astype(jnp.bfloat16)


def factor_level(front_block, level_depth):
    tile_size = lax.axis_size(TILE)
    groups = lax.axis_size("cube") // 2**level_depth
    pivot_tile = 2 - level_depth
    member = lax.axis_index("cube") % groups
    column_dev = lax.axis_index(TILE)
    tile_rows, tile_width, col_tiles, _ = front_block.shape
    pivot_member = pivot_tile % groups
    pivot_row = pivot_tile // groups
    pivot_dev = pivot_tile % tile_size
    pivot_col = pivot_tile // tile_size
    row_ids = jnp.arange(tile_rows, dtype=jnp.int32) * groups + member
    local_strip = front_block[:, :, pivot_col, :]
    own_column = column_dev == pivot_dev
    corner = jnp.where((member == pivot_member) & own_column, local_strip[pivot_row], 0.0)
    corner = spread_corner(corner, groups)
    identity = jnp.eye(tile_width, dtype=jnp.float32)
    corner = jnp.where(own_column, corner, identity)
    own_rows = solve_strip(local_strip, corner, row_ids, pivot_tile)
    factor_rows = from_root(own_rows, TILE, pivot_dev)
    slice_rows = tile_width // tile_size
    panel_part = lax.dynamic_slice_in_dim(factor_rows, column_dev * slice_rows, slice_rows, 1)
    zeroed = jnp.where(
        (row_ids == pivot_tile)[:, None, None], jnp.zeros_like(factor_rows), factor_rows
    )
    col_ids = jnp.arange(col_tiles, dtype=jnp.int32) * tile_size + column_dev
    picked = jnp.take(zeroed, col_ids // groups, axis=0)
    owned_mask = col_ids % groups == member
    picked = jnp.where(owned_mask[:, None, None], picked, jnp.zeros_like(picked))
    col_factor = spread_columns(picked, groups)
    update = jnp.einsum("rik,cjk->ricj", zeroed, col_factor, preferred_element_type=jnp.float32)
    return (panel_part[:, None], front_block - update)


def permute_tiles(block, row_ids, col_ids, perm_table):
    tile_width = block.shape[1]
    slot_ids = jnp.arange(tile_width, dtype=jnp.int32)
    row_perm = jnp.take(perm_table, row_ids, axis=0)
    col_perm = jnp.take(perm_table, col_ids, axis=0)
    row_onehot = (row_perm[:, None, :] == slot_ids[None, :, None]).astype(jnp.float32)
    col_onehot = (col_perm[:, None, :] == slot_ids[None, :, None]).astype(jnp.float32)
    placed = jnp.einsum("rji,ricy->rjcy", row_onehot, block, precision=lax.Precision.HIGHEST)
    return jnp.einsum("rjcy,cly->rjcl", placed, col_onehot, precision=lax.Precision.HIGHEST)


def send_up(schur_block, level_depth, order_table, scatter_table):
    tile_size = lax.axis_size(TILE)
    groups = lax.axis_size("cube") // 2**level_depth
    pivot_tile = 2 - level_depth
    cube_index = lax.axis_index("cube")
    front_id = cube_index // groups
    member = cube_index % groups
    column_dev = lax.axis_index(TILE)
    tile_rows, tile_width, col_tiles, _ = schur_block.shape
    row_ids = jnp.arange(tile_rows, dtype=jnp.int32) * groups + member
    col_ids = jnp.arange(col_tiles, dtype=jnp.int32) * tile_size + column_dev
    offsets = jnp.arange(tile_width, dtype=jnp.int32)
    live_order = order_table[front_id]
    row_keep = (row_ids[:, None] * tile_width + offsets[None, :] < live_order) & (
        row_ids[:, None] != pivot_tile
    )
    col_keep = (col_ids[:, None] * tile_width + offsets[None, :] < live_order) & (
        col_ids[:, None] != pivot_tile
    )
    keep_both = row_keep[:, :, None, None] & col_keep[None, None, :, :]
    masked = jnp.where(keep_both, schur_block, 0.0)
    parity = front_id % 2
    which_bit = groups.bit_length() - 1
    pair_shape = (tile_rows // 2, 2, tile_width, col_tiles, tile_width)
    tile_pairs = masked.reshape(pair_shape)
    kept_half = jnp.where(parity == 0, tile_pairs[:, 0], tile_pairs[:, 1])
    sent_half = jnp.where(parity == 0, tile_pairs[:, 1], tile_pairs[:, 0])
    received = partner_2(sent_half, "cube", which_bit)
    kept_ids = (jnp.arange(tile_rows // 2, dtype=jnp.int32) * 2 + parity) * groups + member
    partner = front_id + 1 - 2 * parity
    own_part = permute_tiles(kept_half, kept_ids, col_ids, scatter_table[front_id])
    other_part = permute_tiles(received, kept_ids, col_ids, scatter_table[partner])
    return own_part + other_part


def per_device(
    leaf_fronts, middle_fronts, root_front, leaf_scatter, middle_scatter, leaf_orders, middle_orders
):
    leaf_panel, leaf_schur = factor_level(leaf_fronts, 2)
    middle_input = middle_fronts + send_up(leaf_schur, 2, leaf_orders, leaf_scatter)
    middle_panel, middle_schur = factor_level(middle_input, 1)
    root_input = root_front + send_up(middle_schur, 1, middle_orders, middle_scatter)
    root_panel, root_schur = factor_level(root_input, 0)
    return (leaf_panel, middle_panel, root_panel, root_schur.astype(jnp.bfloat16))


def solution(mesh):
    split = Mesh(mesh.devices.reshape(mesh.shape["cube"], 4, 8), ("cube", "tile_0", "tile_1"))
    placed = (
        P(None, "cube", None, TILE),
        P(None, "cube", None, TILE),
        P(None, "cube", None, TILE),
        P(),
        P(),
        P(),
        P(),
    )
    return jax.shard_map(
        per_device,
        mesh=split,
        in_specs=placed,
        out_specs=(
            P(None, "cube", TILE, None),
            P(None, "cube", TILE, None),
            P(None, "cube", TILE, None),
            P(None, "cube", None, TILE),
        ),
        check_vma=False,
    )
```

profile of v0, /device:TPU:12, one launch (start us, length us, event | category | flops | bytes accessed | tf_op | source)
XLA Modules:
  0.0 1045.2 jit_solution(14356378276181455765)
XLA Ops:
  12.2 15.7 %collective-permute-start.1 = (f32[256,256]{0,1:T(8,128)S(1)}, f32[256,256]{0,1:T(8,128)S(1)}, u32[]{:S(2)}, u32[]{:S(2)}) collective-permute-start(f32[256,256]{0,1:T(8,128)S(1)} %fusion.113), channel_id=1, source_target_pairs={{0,64},{64,0},{32,96},{96,32},{128,192},{192,128},{160,224},{224,1... | collective-permute-start | bytes 786440 | tf_op jit(solution)/shard_map/ppermute | solution.py:17
  29.5 5.3 collective-permute-done.1
  35.0 11.7 %cholesky.172 = f32[128,128]{1,0:T(8,128)S(1)} custom-call(f32[128,128]{1,0:T(8,128)S(1)} %cholesky.270), custom_call_target="Cholesky" | custom-call | tf_op jit(solution)/shard_map/jit(cholesky)/cholesky | solution.py:46
  46.8 9.8 custom-call.25
  57.1 11.7 %cholesky.189 = f32[128,128]{1,0:T(8,128)S(1)} custom-call(f32[128,128]{1,0:T(8,128)S(1)} %convolution_subtract_fusion.5), custom_call_target="Cholesky" | custom-call | tf_op jit(solution)/shard_map/jit(cholesky)/cholesky | solution.py:46
  70.9 4.1 while.7
  75.1 19.7 %custom-call.20 = f32[2,128,128]{1,2,0:T(8,128)S(1)} custom-call(f32[2,128,128]{2,1,0:T(8,128)S(1)} %get-tuple-element.23), custom_call_target="InvertDiagBlocksLowerTriangular" | custom-call | tf_op jit(solution)/shard_map/jit(_solve_triangular)/triangular_solve | solution.py:48
  100.6 78.1 %all-reduce.8.cloned.1.call-done = bf16[8,256,256]{2,1,0:T(8,128)(2,1)} async-done(((bf16[8,256,256]{2,1,0:T(8,128)(2,1)}), bf16[8,256,256]{2,1,0:T(8,128)(2,1)}) %all-reduce.8.cloned.1.call-update) | async-done | bytes 1048592 | tf_op jit(solution)/shard_map/psum | solution.py:23
  179.4 132.8 %all-reduce.10.cloned.1.call-done = bf16[8,256,256]{2,1,0:T(8,128)(2,1)} async-done(((bf16[8,256,256]{2,1,0:T(8,128)(2,1)}), bf16[8,256,256]{2,1,0:T(8,128)(2,1)}) %all-reduce.10.cloned.1.call-update) | async-done | bytes 1048592 | tf_op jit(solution)/shard_map/psum | solution.py:23
  316.8 5.1 collective-permute-start.3
  322.7 11.3 %collective-permute-done.3 = bf16[1,256,256]{2,1,0:T(8,128)(2,1)S(1)} collective-permute-done((bf16[1,256,256]{2,1,0:T(8,128)(2,1)S(1)}, bf16[1,256,256]{2,1,0:T(8,128)(2,1)S(1)}, u32[]{:S(2)}, u32[]{:S(2)}) %collective-permute-start.3) | collective-permute-done | bytes 131104 | tf_op jit(solution)/shard_map/ppermute | solution.py:17
  337.4 3.1 collective-permute-start.4
  345.6 19.1 %collective-permute-done.4 = f32[4,256,1,256]{3,1,0,2:T(8,128)} collective-permute-done((f32[4,256,1,256]{3,1,0,2:T(8,128)}, f32[4,256,1,256]{3,1,0,2:T(8,128)}, u32[]{:S(2)}, u32[]{:S(2)}) %collective-permute-start.4) | collective-permute-done | bytes 1048608 | tf_op jit(solution)/shard_map/ppermute | solution.py:17
  370.9 9.2 collective-permute-start.6
  380.1 15.8 %collective-permute-done.6 = f32[256,256]{0,1:T(8,128)S(1)} collective-permute-done((f32[256,256]{0,1:T(8,128)S(1)}, f32[256,256]{0,1:T(8,128)S(1)}, u32[]{:S(2)}, u32[]{:S(2)}) %collective-permute-start.6) | collective-permute-done | bytes 262176 | tf_op jit(solution)/shard_map/ppermute | solution.py:17
  395.9 3.3 collective-permute-start.7
  399.5 6.4 collective-permute-done.7
  406.2 11.7 %cholesky.206 = f32[128,128]{1,0:T(8,128)S(1)} custom-call(f32[128,128]{1,0:T(8,128)S(1)} %cholesky.273), custom_call_target="Cholesky" | custom-call | tf_op jit(solution)/shard_map/jit(cholesky)/cholesky | solution.py:46
  418.0 9.8 custom-call.26
  428.3 11.7 %cholesky.223 = f32[128,128]{1,0:T(8,128)S(1)} custom-call(f32[128,128]{1,0:T(8,128)S(1)} %convolution_subtract_fusion.4), custom_call_target="Cholesky" | custom-call | tf_op jit(solution)/shard_map/jit(cholesky)/cholesky | solution.py:46
  442.8 4.4 while.8
  447.2 19.7 %custom-call.21 = f32[2,128,128]{1,2,0:T(8,128)S(1)} custom-call(f32[2,128,128]{2,1,0:T(8,128)S(1)} %get-tuple-element.39), custom_call_target="InvertDiagBlocksLowerTriangular" | custom-call | tf_op jit(solution)/shard_map/jit(_solve_triangular)/triangular_solve | solution.py:48
  470.6 57.2 %all-reduce.12.cloned.1.call-done = bf16[4,256,256]{2,1,0:T(8,128)(2,1)} async-done(((bf16[4,256,256]{2,1,0:T(8,128)(2,1)}), bf16[4,256,256]{2,1,0:T(8,128)(2,1)}) %all-reduce.12.cloned.1.call-update) | async-done | bytes 524304 | tf_op jit(solution)/shard_map/psum | solution.py:23
  529.1 126.9 %all-reduce.14.cloned.1.call-done = bf16[4,256,256]{2,1,0:T(8,128)(2,1)} async-done(((bf16[4,256,256]{2,1,0:T(8,128)(2,1)}), bf16[4,256,256]{2,1,0:T(8,128)(2,1)}) %all-reduce.14.cloned.1.call-update) | async-done | bytes 524304 | tf_op jit(solution)/shard_map/psum | solution.py:23
  660.5 5.2 collective-permute-start.9
  666.4 11.7 %collective-permute-done.9 = bf16[1,256,256]{2,1,0:T(8,128)(2,1)S(1)} collective-permute-done((bf16[1,256,256]{2,1,0:T(8,128)(2,1)S(1)}, bf16[1,256,256]{2,1,0:T(8,128)(2,1)S(1)}, u32[]{:S(2)}, u32[]{:S(2)}) %collective-permute-start.9) | collective-permute-done | bytes 131104 | tf_op jit(solution)/shard_map/ppermute | solution.py:17
  678.1 3.1 collective-permute-start.10
  681.9 3.5 collective-permute-done.10
  686.7 2.4 collective-permute-start.11
  690.5 12.8 %collective-permute-done.11 = f32[2,256,1,256]{1,3,0,2:T(8,128)S(1)} collective-permute-done((f32[2,256,1,256]{1,3,0,2:T(8,128)}, f32[2,256,1,256]{1,3,0,2:T(8,128)S(1)}, u32[]{:S(2)}, u32[]{:S(2)}) %collective-permute-start.11) | collective-permute-done | bytes 524320 | tf_op jit(solution)/shard_map/ppermute | solution.py:17
  707.8 8.0 collective-permute-start.13
  715.7 16.6 %collective-permute-done.13 = f32[256,256]{0,1:T(8,128)S(1)} collective-permute-done((f32[256,256]{0,1:T(8,128)S(1)}, f32[256,256]{0,1:T(8,128)S(1)}, u32[]{:S(2)}, u32[]{:S(2)}) %collective-permute-start.13) | collective-permute-done | bytes 262176 | tf_op jit(solution)/shard_map/ppermute | solution.py:17
  732.4 3.1 collective-permute-start.14
  735.5 7.1 collective-permute-done.14
  742.6 2.6 collective-permute-start.15
  745.4 7.9 collective-permute-done.15
  753.6 11.7 %cholesky.240 = f32[128,128]{1,0:T(8,128)S(1)} custom-call(f32[128,128]{1,0:T(8,128)S(1)} %cholesky.276), custom_call_target="Cholesky" | custom-call | tf_op jit(solution)/shard_map/jit(cholesky)/cholesky | solution.py:46
  765.4 9.8 custom-call.27
  775.7 11.7 %cholesky.257 = f32[128,128]{1,0:T(8,128)S(1)} custom-call(f32[128,128]{1,0:T(8,128)S(1)} %convolution_subtract_fusion.3), custom_call_target="Cholesky" | custom-call | tf_op jit(solution)/shard_map/jit(cholesky)/cholesky | solution.py:46
  790.2 4.3 while.9
  794.5 19.7 %custom-call.22 = f32[2,128,128]{1,2,0:T(8,128)S(1)} custom-call(f32[2,128,128]{2,1,0:T(8,128)S(1)} %get-tuple-element.55), custom_call_target="InvertDiagBlocksLowerTriangular" | custom-call | tf_op jit(solution)/shard_map/jit(_solve_triangular)/triangular_solve | solution.py:48
  816.6 55.5 %all-reduce.16.cloned.1.call-done = bf16[2,256,256]{2,1,0:T(8,128)(2,1)} async-done(((bf16[2,256,256]{2,1,0:T(8,128)(2,1)}), bf16[2,256,256]{2,1,0:T(8,128)(2,1)}) %all-reduce.16.cloned.1.call-update) | async-done | bytes 262160 | tf_op jit(solution)/shard_map/psum | solution.py:23
  872.2 126.7 %all-reduce.18.cloned.1.call-done = bf16[2,256,256]{2,1,0:T(8,128)(2,1)} async-done(((bf16[2,256,256]{2,1,0:T(8,128)(2,1)}), bf16[2,256,256]{2,1,0:T(8,128)(2,1)}) %all-reduce.18.cloned.1.call-update) | async-done | bytes 262160 | tf_op jit(solution)/shard_map/psum | solution.py:23
  1003.3 5.3 collective-permute-start.17
  1008.6 12.6 %collective-permute-done.17 = bf16[1,256,256]{2,1,0:T(8,128)(2,1)S(1)} collective-permute-done((bf16[1,256,256]{2,1,0:T(8,128)(2,1)S(1)}, bf16[1,256,256]{2,1,0:T(8,128)(2,1)S(1)}, u32[]{:S(2)}, u32[]{:S(2)}) %collective-permute-start.17) | collective-permute-done | bytes 131104 | tf_op jit(solution)/shard_map/ppermute | solution.py:17
  1021.2 3.1 collective-permute-start.18
  1025.7 2.9 collective-permute-done.18
  1033.6 3.4 collective-permute-done.19
  (189 shorter events, 83.3 us)
Async XLA Ops:
  7.2 20.7 %copy-start = (f32[8,256,1,256]{3,2,1,0:T(1,128)S(1)}, f32[8,256,1,256]{3,2,1,0:T(1,128)}, u32[]{:S(2)}) copy-start(f32[8,256,1,256]{3,2,1,0:T(1,128)} %param.14) | copy-start | bytes 6291460
  7.2 171.5 %all-reduce.8.cloned.1.call-start = ((), (), s32[]{:S(2)}) async-start(), calls=%async_computation | async-start | bytes 2097152 | tf_op jit(solution)/shard_map/psum | solution.py:23
  8.7 3.4 collective-permute-start
  12.2 22.6 %collective-permute-start.1 = (f32[256,256]{0,1:T(8,128)S(1)}, f32[256,256]{0,1:T(8,128)S(1)}, u32[]{:S(2)}, u32[]{:S(2)}) collective-permute-start(f32[256,256]{0,1:T(8,128)S(1)} %fusion.113), channel_id=1, source_target_pairs={{0,64},{64,0},{32,96},{96,32},{128,192},{192,128},{160,224},{224,1... | collective-permute-start | bytes 786440 | tf_op jit(solution)/shard_map/ppermute | solution.py:17
  34.8 59.9 %copy-start.1 = (f32[8,256,1,256]{3,1,2,0:T(8,128)S(1)}, f32[8,256,1,256]{3,1,2,0:T(8,128)}, u32[]{:S(2)}) copy-start(f32[8,256,1,256]{3,1,2,0:T(8,128)} %copy.56) | copy-start | bytes 6291460
  99.4 79.4 %copy-start.5 = (s32[4]{0:T(128)S(1)}, s32[4]{0:T(128)}, u32[]{:S(2)}) copy-start(s32[4]{0:T(128)} %param.19) | copy-start | bytes 52
  100.6 222.1 %copy-start.4 = (s32[4,32,256]{2,1,0:T(8,128)S(1)}, s32[4,32,256]{2,1,0:T(8,128)}, u32[]{:S(2)}) copy-start(s32[4,32,256]{2,1,0:T(8,128)} %param.17) | copy-start | bytes 393220
  100.6 211.6 %all-reduce.10.cloned.1.call-start = ((), (), s32[]{:S(2)}) async-start(), calls=%async_computation.1 | async-start | bytes 2097152 | tf_op jit(solution)/shard_map/psum | solution.py:23
  178.7 349.0 %all-reduce.12.cloned.1.call-start = ((), (), s32[]{:S(2)}) async-start(), calls=%async_computation.2 | async-start | bytes 1048576 | tf_op jit(solution)/shard_map/psum | solution.py:23
  313.6 3.2 collective-permute-start.2
  316.8 17.1 %collective-permute-start.3 = (bf16[1,256,256]{2,1,0:T(8,128)(2,1)S(1)}, bf16[1,256,256]{2,1,0:T(8,128)(2,1)S(1)}, u32[]{:S(2)}, u32[]{:S(2)}) collective-permute-start(bf16[1,256,256]{2,1,0:T(8,128)(2,1)S(1)} %fusion.112), channel_id=1, source_target_pairs={{0,64},{64,0},{32,96},{96,32},{128,192},{192,128},{160,224},{224,1... | collective-permute-start | bytes 393224 | tf_op jit(solution)/shard_map/ppermute | solution.py:17
  337.4 27.3 %collective-permute-start.4 = (f32[4,256,1,256]{3,1,0,2:T(8,128)}, f32[4,256,1,256]{3,1,0,2:T(8,128)}, u32[]{:S(2)}, u32[]{:S(2)}) collective-permute-start(f32[4,256,1,256]{3,1,0,2:T(8,128)} %select_bitcast_fusion), channel_id=1, source_target_pairs={{0,128},{128,0},{32,160},{160,32},{64,192},{192,64},{96,224},{224,... | collective-permute-start | bytes 3145736 | tf_op jit(solution)/shard_map/ppermute | solution.py:17
  367.4 3.4 collective-permute-start.5
  370.9 24.9 %collective-permute-start.6 = (f32[256,256]{0,1:T(8,128)S(1)}, f32[256,256]{0,1:T(8,128)S(1)}, u32[]{:S(2)}, u32[]{:S(2)}) collective-permute-start(f32[256,256]{0,1:T(8,128)S(1)} %fusion.111), channel_id=1, source_target_pairs={{0,64},{64,0},{32,96},{96,32},{128,192},{192,128},{160,224},{224,1... | collective-permute-start | bytes 786440 | tf_op jit(solution)/shard_map/ppermute | solution.py:17
  395.9 10.1 collective-permute-start.7
  469.2 58.7 %copy-start.3 = (s32[2,32,256]{2,1,0:T(8,128)S(1)}, s32[2,32,256]{2,1,0:T(8,128)}, u32[]{:S(2)}) copy-start(s32[2,32,256]{2,1,0:T(8,128)} %param.18) | copy-start | bytes 196612
  469.5 189.7 %copy-start.6 = (s32[2]{0:T(128)S(1)}, s32[2]{0:T(128)}, u32[]{:S(2)}) copy-start(s32[2]{0:T(128)} %param.20) | copy-start | bytes 28
  470.4 185.6 %all-reduce.14.cloned.1.call-start = ((), (), s32[]{:S(2)}) async-start(), calls=%async_computation.3 | async-start | bytes 1048576 | tf_op jit(solution)/shard_map/psum | solution.py:23
  527.8 344.4 %all-reduce.16.cloned.1.call-start = ((), (), s32[]{:S(2)}) async-start(), calls=%async_computation.4 | async-start | bytes 524288 | tf_op jit(solution)/shard_map/psum | solution.py:23
  657.2 3.2 collective-permute-start.8
  660.5 17.6 %collective-permute-start.9 = (bf16[1,256,256]{2,1,0:T(8,128)(2,1)S(1)}, bf16[1,256,256]{2,1,0:T(8,128)(2,1)S(1)}, u32[]{:S(2)}, u32[]{:S(2)}) collective-permute-start(bf16[1,256,256]{2,1,0:T(8,128)(2,1)S(1)} %fusion.110), channel_id=1, source_target_pairs={{0,64},{64,0},{32,96},{96,32},{128,192},{192,128},{160,224},{224,1... | collective-permute-start | bytes 393224 | tf_op jit(solution)/shard_map/ppermute | solution.py:17
  678.1 7.3 collective-permute-start.10
  681.9 7.3 copy-start.2
  686.7 16.6 %collective-permute-start.11 = (f32[2,256,1,256]{1,3,0,2:T(8,128)}, f32[2,256,1,256]{1,3,0,2:T(8,128)S(1)}, u32[]{:S(2)}, u32[]{:S(2)}) collective-permute-start(f32[2,256,1,256]{1,3,0,2:T(8,128)} %select_bitcast_fusion.1), channel_id=1, source_target_pairs={{0,256},{256,0},{32,288},{288,32},{64,320},{320,64},{96,352},{352,... | collective-permute-start | bytes 1572872 | tf_op jit(solution)/shard_map/ppermute | solution.py:17
  704.3 3.4 collective-permute-start.12
  707.8 24.6 %collective-permute-start.13 = (f32[256,256]{0,1:T(8,128)S(1)}, f32[256,256]{0,1:T(8,128)S(1)}, u32[]{:S(2)}, u32[]{:S(2)}) collective-permute-start(f32[256,256]{0,1:T(8,128)S(1)} %fusion.109), channel_id=1, source_target_pairs={{0,64},{64,0},{32,96},{96,32},{128,192},{192,128},{160,224},{224,1... | collective-permute-start | bytes 786440 | tf_op jit(solution)/shard_map/ppermute | solution.py:17
  732.4 10.1 collective-permute-start.14
  742.6 10.8 %collective-permute-start.15 = (f32[256,256]{0,1:T(8,128)S(1)}, f32[256,256]{0,1:T(8,128)S(1)}, u32[]{:S(2)}, u32[]{:S(2)}) collective-permute-start(f32[256,256]{0,1:T(8,128)S(1)} %add.403), channel_id=1, source_target_pairs={{0,256},{256,0},{32,288},{288,32},{64,320},{320,64},{96,352},{352,... | collective-permute-start | bytes 786440 | tf_op jit(solution)/shard_map/ppermute | solution.py:17
  816.6 182.3 %all-reduce.18.cloned.1.call-start = ((), (), s32[]{:S(2)}) async-start(), calls=%async_computation.5 | async-start | bytes 524288 | tf_op jit(solution)/shard_map/psum | solution.py:23
  1000.0 3.2 collective-permute-start.16
  1003.3 17.9 %collective-permute-start.17 = (bf16[1,256,256]{2,1,0:T(8,128)(2,1)S(1)}, bf16[1,256,256]{2,1,0:T(8,128)(2,1)S(1)}, u32[]{:S(2)}, u32[]{:S(2)}) collective-permute-start(bf16[1,256,256]{2,1,0:T(8,128)(2,1)S(1)} %fusion.108), channel_id=1, source_target_pairs={{0,64},{64,0},{32,96},{96,32},{128,192},{192,128},{160,224},{224,1... | collective-permute-start | bytes 393224 | tf_op jit(solution)/shard_map/ppermute | solution.py:17
  1021.2 7.3 collective-permute-start.18
  1028.6 8.4 collective-permute-start.19
Sparse Core Ops, SparseCore 0:
  100.7 77.9 all-reduce.7
  181.6 130.5 all-reduce.9
  470.6 57.1 all-reduce.11
  530.5 125.4 all-reduce.13
  816.7 55.4 all-reduce.15
  874.9 123.9 all-reduce.17
where the time goes:
time: 1050 us
  waiting for transfers between devices  721 us (69%)
  other arithmetic  175 us (17%)
  starting transfers between devices  83.2 us (8%)
  local copies, waits for them, and re-layouts  27.9 us (3%)
  between operations  19.5 us (2%)
  matrix products  18 us (2%)
    psum x6, waiting for transfers between devices, from_root(): value = lax.psum(value, axis)  577 us
    ppermute x20, waiting for transfers between devices, partner_2(): return lax.ppermute(block, axis, route)  143 us
    another operation x20, other arithmetic, solve_strip(): lower_factor = jnp.linalg.cholesky(corner)  103 us
    ppermute x20, starting transfers between devices, partner_2(): return lax.ppermute(block, axis, route)  83 us
    another operation x7, other arithmetic, solve_strip(): jax.scipy.linalg.solve_triangular(lower_factor, flat_strip.T, lower=True)  59.1 us
  transfers between devices with their start and end apart: 26, of which 26 were waited for; matrix products, arithmetic and copies ran while one was open for 2% of the time, Pallas kernels for 0%

commit v1 on v0

--- a/solution.py
+++ b/solution.py
@@ -20,7 +20,8 @@
 def from_root(value, axes, root):
     value = jnp.where(lax.axis_index(axes) == root, value, jnp.zeros_like(value))
     for axis in axes:
-        value = lax.psum(value, axis)
+        parts = lax.all_gather(value, axis)
+        value = jnp.sum(parts, axis=0)
     return value
 
 

time: 1050 us -> 1010 us (0.962)
  the two profiles are of different devices: /device:TPU:12 before, /device:TPU:4 now
where the time goes in v1:
time: 1010 us; the launch traced here: 997 us
  waiting for transfers between devices  656 us (65%)
  other arithmetic  192 us (19%)
  starting transfers between devices  83.1 us (8%)
  local copies, waits for them, and re-layouts  28.8 us (3%)
  between operations  19.5 us (2%)
  matrix products  17.5 us (2%)
    all_gather x6, waiting for transfers between devices, from_root(): parts = lax.all_gather(value, axis)  496 us
    ppermute x20, waiting for transfers between devices, partner_2(): return lax.ppermute(block, axis, route)  160 us
    another operation x20, other arithmetic, solve_strip(): lower_factor = jnp.linalg.cholesky(corner)  103 us
    ppermute x20, starting transfers between devices, partner_2(): return lax.ppermute(block, axis, route)  82.8 us
    another operation x7, other arithmetic, solve_strip(): jax.scipy.linalg.solve_triangular(lower_factor, flat_strip.T, lower=True)  59.3 us
  transfers between devices with their start and end apart: 26, of which 26 were waited for; matrix products, arithmetic and copies ran while one was open for 2% of the time, Pallas kernels for 0%

profile of v1, /device:TPU:4, one launch (start us, length us, event | category | flops | bytes accessed | tf_op | source)
XLA Modules:
  0.0 997.2 jit_solution(7111754305175341370)
XLA Ops:
  12.2 15.7 %collective-permute-start.1 = (f32[256,256]{0,1:T(8,128)S(1)}, f32[256,256]{0,1:T(8,128)S(1)}, u32[]{:S(2)}, u32[]{:S(2)}) collective-permute-start(f32[256,256]{0,1:T(8,128)S(1)} %fusion.110), channel_id=1, source_target_pairs={{0,64},{64,0},{32,96},{96,32},{128,192},{192,128},{160,224},{224,1... | collective-permute-start | bytes 786440 | tf_op jit(solution)/shard_map/ppermute | solution.py:17
  31.4 3.4 collective-permute-done.1
  35.0 11.7 %cholesky.172 = f32[128,128]{1,0:T(8,128)S(1)} custom-call(f32[128,128]{1,0:T(8,128)S(1)} %cholesky.270), custom_call_target="Cholesky" | custom-call | tf_op jit(solution)/shard_map/jit(cholesky)/cholesky | solution.py:47
  46.8 9.8 custom-call.25
  57.1 11.7 %cholesky.189 = f32[128,128]{1,0:T(8,128)S(1)} custom-call(f32[128,128]{1,0:T(8,128)S(1)} %convolution_subtract_fusion.5), custom_call_target="Cholesky" | custom-call | tf_op jit(solution)/shard_map/jit(cholesky)/cholesky | solution.py:47
  70.8 3.8 while.7
  74.6 19.9 %custom-call.20 = f32[2,128,128]{1,2,0:T(8,128)S(1)} custom-call(f32[2,128,128]{2,1,0:T(8,128)S(1)} %get-tuple-element.23), custom_call_target="InvertDiagBlocksLowerTriangular" | custom-call | tf_op jit(solution)/shard_map/jit(_solve_triangular)/triangular_solve | solution.py:49
  99.5 73.2 %all-gather.10.cloned.1.call-done = bf16[4,8,256,256]{3,2,1,0:T(8,128)(2,1)} async-done(((bf16[1,8,256,256]{3,2,1,0:T(8,128)(2,1)}), bf16[4,8,256,256]{3,2,1,0:T(8,128)(2,1)}) %all-gather.10.cloned.1.call-update) | async-done | bytes 4194320 | tf_op jit(solution)/shard_map/all_gather | solution.py:23
  172.7 4.2 reduce_sum.72
  177.7 181.8 %all-gather.16.cloned.1.call-done = bf16[64,256,256]{2,1,0:T(8,128)(2,1)} async-done(((bf16[8,256,256]{2,1,0:T(8,128)(2,1)}), bf16[64,256,256]{2,1,0:T(8,128)(2,1)}) %all-gather.16.cloned.1.call-update) | async-done | bytes 8388624 | tf_op jit(solution)/shard_map/all_gather | solution.py:23
  359.5 5.0 reduce_sum.73
  368.1 6.0 collective-permute-start.3
  374.8 16.5 %collective-permute-done.3 = bf16[1,256,256]{2,1,0:T(8,128)(2,1)S(1)} collective-permute-done((bf16[1,256,256]{2,1,0:T(8,128)(2,1)S(1)}, bf16[1,256,256]{2,1,0:T(8,128)(2,1)S(1)}, u32[]{:S(2)}, u32[]{:S(2)}) %collective-permute-start.3) | collective-permute-done | bytes 131104 | tf_op jit(solution)/shard_map/ppermute | solution.py:17
  394.7 3.1 collective-permute-start.4
  402.9 19.0 %collective-permute-done.4 = f32[4,256,1,256]{3,1,0,2:T(8,128)} collective-permute-done((f32[4,256,1,256]{3,1,0,2:T(8,128)}, f32[4,256,1,256]{3,1,0,2:T(8,128)}, u32[]{:S(2)}, u32[]{:S(2)}) %collective-permute-start.4) | collective-permute-done | bytes 1048608 | tf_op jit(solution)/shard_map/ppermute | solution.py:17
  428.2 5.1 collective-permute-start.6
  433.3 22.0 %collective-permute-done.6 = f32[256,256]{0,1:T(8,128)S(1)} collective-permute-done((f32[256,256]{0,1:T(8,128)S(1)}, f32[256,256]{0,1:T(8,128)S(1)}, u32[]{:S(2)}, u32[]{:S(2)}) %collective-permute-start.6) | collective-permute-done | bytes 262176 | tf_op jit(solution)/shard_map/ppermute | solution.py:17
  455.3 3.5 collective-permute-start.7
  459.5 6.1 collective-permute-done.7
  466.8 11.7 %cholesky.206 = f32[128,128]{1,0:T(8,128)S(1)} custom-call(f32[128,128]{1,0:T(8,128)S(1)} %cholesky.273), custom_call_target="Cholesky" | custom-call | tf_op jit(solution)/shard_map/jit(cholesky)/cholesky | solution.py:47
  478.5 9.8 custom-call.26
  488.8 11.7 %cholesky.223 = f32[128,128]{1,0:T(8,128)S(1)} custom-call(f32[128,128]{1,0:T(8,128)S(1)} %convolution_subtract_fusion.4), custom_call_target="Cholesky" | custom-call | tf_op jit(solution)/shard_map/jit(cholesky)/cholesky | solution.py:47
  503.2 4.1 while.8
  507.3 19.7 %custom-call.21 = f32[2,128,128]{1,2,0:T(8,128)S(1)} custom-call(f32[2,128,128]{2,1,0:T(8,128)S(1)} %get-tuple-element.39), custom_call_target="InvertDiagBlocksLowerTriangular" | custom-call | tf_op jit(solution)/shard_map/jit(_solve_triangular)/triangular_solve | solution.py:49
  530.2 36.4 %all-gather.12.cloned.1.call-done = bf16[4,4,256,256]{3,2,1,0:T(8,128)(2,1)} async-done(((bf16[1,4,256,256]{3,2,1,0:T(8,128)(2,1)}), bf16[4,4,256,256]{3,2,1,0:T(8,128)(2,1)}) %all-gather.12.cloned.1.call-update) | async-done | bytes 2097168 | tf_op jit(solution)/shard_map/all_gather | solution.py:23
  566.6 2.9 reduce_sum.74
  570.8 102.4 %all-gather.18.cloned.1.call-done = bf16[32,256,256]{2,1,0:T(8,128)(2,1)} async-done(((bf16[4,256,256]{2,1,0:T(8,128)(2,1)}), bf16[32,256,256]{2,1,0:T(8,128)(2,1)}) %all-gather.18.cloned.1.call-update) | async-done | bytes 4194320 | tf_op jit(solution)/shard_map/all_gather | solution.py:23
  679.5 5.8 collective-permute-start.9
  686.0 15.4 %collective-permute-done.9 = bf16[1,256,256]{2,1,0:T(8,128)(2,1)S(1)} collective-permute-done((bf16[1,256,256]{2,1,0:T(8,128)(2,1)S(1)}, bf16[1,256,256]{2,1,0:T(8,128)(2,1)S(1)}, u32[]{:S(2)}, u32[]{:S(2)}) %collective-permute-start.9) | collective-permute-done | bytes 131104 | tf_op jit(solution)/shard_map/ppermute | solution.py:17
  701.4 3.1 collective-permute-start.10
  705.2 3.6 collective-permute-done.10
  714.3 12.9 %collective-permute-done.11 = f32[2,256,1,256]{3,1,0,2:T(8,128)} collective-permute-done((f32[2,256,1,256]{3,1,0,2:T(8,128)}, f32[2,256,1,256]{3,1,0,2:T(8,128)}, u32[]{:S(2)}, u32[]{:S(2)}) %collective-permute-start.11) | collective-permute-done | bytes 524320 | tf_op jit(solution)/shard_map/ppermute | solution.py:17
  732.6 7.8 collective-permute-start.13
  740.4 19.6 %collective-permute-done.13 = f32[256,256]{0,1:T(8,128)S(1)} collective-permute-done((f32[256,256]{0,1:T(8,128)S(1)}, f32[256,256]{0,1:T(8,128)S(1)}, u32[]{:S(2)}, u32[]{:S(2)}) %collective-permute-start.13) | collective-permute-done | bytes 262176 | tf_op jit(solution)/shard_map/ppermute | solution.py:17
  760.1 3.1 collective-permute-start.14
  763.2 7.0 collective-permute-done.14
  773.4 7.7 collective-permute-done.15
  781.3 11.7 %cholesky.240 = f32[128,128]{1,0:T(8,128)S(1)} custom-call(f32[128,128]{1,0:T(8,128)S(1)} %cholesky.276), custom_call_target="Cholesky" | custom-call | tf_op jit(solution)/shard_map/jit(cholesky)/cholesky | solution.py:47
  793.1 9.8 custom-call.27
  803.4 11.7 %cholesky.257 = f32[128,128]{1,0:T(8,128)S(1)} custom-call(f32[128,128]{1,0:T(8,128)S(1)} %convolution_subtract_fusion.3), custom_call_target="Cholesky" | custom-call | tf_op jit(solution)/shard_map/jit(cholesky)/cholesky | solution.py:47
  817.6 4.1 while.9
  821.7 19.7 %custom-call.22 = f32[2,128,128]{1,2,0:T(8,128)S(1)} custom-call(f32[2,128,128]{2,1,0:T(8,128)S(1)} %get-tuple-element.55), custom_call_target="InvertDiagBlocksLowerTriangular" | custom-call | tf_op jit(solution)/shard_map/jit(_solve_triangular)/triangular_solve | solution.py:49
  843.7 30.7 %all-gather.14.cloned.1.call-done = bf16[4,2,256,256]{3,2,1,0:T(8,128)(2,1)} async-done(((bf16[1,2,256,256]{3,2,1,0:T(8,128)(2,1)}), bf16[4,2,256,256]{3,2,1,0:T(8,128)(2,1)}) %all-gather.14.cloned.1.call-update) | async-done | bytes 1048592 | tf_op jit(solution)/shard_map/all_gather | solution.py:23
  876.6 71.0 %all-gather.20.cloned.1.call-done = bf16[16,256,256]{2,1,0:T(8,128)(2,1)} async-done(((bf16[2,256,256]{2,1,0:T(8,128)(2,1)}), bf16[16,256,256]{2,1,0:T(8,128)(2,1)}) %all-gather.20.cloned.1.call-update) | async-done | bytes 2097168 | tf_op jit(solution)/shard_map/all_gather | solution.py:23
  952.9 7.5 collective-permute-start.17
  960.5 12.6 %collective-permute-done.17 = bf16[1,256,256]{2,1,0:T(8,128)(2,1)S(1)} collective-permute-done((bf16[1,256,256]{2,1,0:T(8,128)(2,1)S(1)}, bf16[1,256,256]{2,1,0:T(8,128)(2,1)S(1)}, u32[]{:S(2)}, u32[]{:S(2)}) %collective-permute-start.17) | collective-permute-done | bytes 131104 | tf_op jit(solution)/shard_map/ppermute | solution.py:17
  973.1 3.0 collective-permute-start.18
  984.1 4.7 collective-permute-done.19
  (201 shorter events, 96.5 us)
Async XLA Ops:
  7.2 20.7 %copy-start = (f32[8,256,1,256]{3,2,1,0:T(1,128)S(1)}, f32[8,256,1,256]{3,2,1,0:T(1,128)}, u32[]{:S(2)}) copy-start(f32[8,256,1,256]{3,2,1,0:T(1,128)} %param.14) | copy-start | bytes 6291460
  7.2 165.5 %all-gather.10.cloned.1.call-start = ((), (), s32[]{:S(2)}) async-start(), calls=%async_computation | async-start | bytes 5242880 | tf_op jit(solution)/shard_map/all_gather | solution.py:23
  8.7 3.4 collective-permute-start
  12.2 22.6 %collective-permute-start.1 = (f32[256,256]{0,1:T(8,128)S(1)}, f32[256,256]{0,1:T(8,128)S(1)}, u32[]{:S(2)}, u32[]{:S(2)}) collective-permute-start(f32[256,256]{0,1:T(8,128)S(1)} %fusion.110), channel_id=1, source_target_pairs={{0,64},{64,0},{32,96},{96,32},{128,192},{192,128},{160,224},{224,1... | collective-permute-start | bytes 786440 | tf_op jit(solution)/shard_map/ppermute | solution.py:17
  99.5 77.6 %copy-start.5 = (s32[4]{0:T(128)S(1)}, s32[4]{0:T(128)}, u32[]{:S(2)}) copy-start(s32[4]{0:T(128)} %param.19) | copy-start | bytes 52
  99.5 260.0 %all-gather.16.cloned.1.call-start = ((), (), s32[]{:S(2)}) async-start(), calls=%async_computation.3 | async-start | bytes 9437184 | tf_op jit(solution)/shard_map/all_gather | solution.py:23
  176.9 389.6 %all-gather.12.cloned.1.call-start = ((), (), s32[]{:S(2)}) async-start(), calls=%async_computation.1 | async-start | bytes 2621440 | tf_op jit(solution)/shard_map/all_gather | solution.py:23
  364.5 10.3 %copy-start.1 = (bf16[8,256,256]{2,1,0:T(8,128)(2,1)}, bf16[8,256,256]{2,1,0:T(8,128)(2,1)S(1)}, u32[]{:S(2)}) copy-start(bf16[8,256,256]{2,1,0:T(8,128)(2,1)S(1)} %reduce_sum.73) | copy-start | bytes 3145732
  364.5 10.2 %copy-start.4 = (s32[4,32,256]{2,1,0:T(8,128)S(1)}, s32[4,32,256]{2,1,0:T(8,128)}, u32[]{:S(2)}) copy-start(s32[4,32,256]{2,1,0:T(8,128)} %param.17) | copy-start | bytes 393220
  364.7 3.4 collective-permute-start.2
  368.1 23.2 %collective-permute-start.3 = (bf16[1,256,256]{2,1,0:T(8,128)(2,1)S(1)}, bf16[1,256,256]{2,1,0:T(8,128)(2,1)S(1)}, u32[]{:S(2)}, u32[]{:S(2)}) collective-permute-start(bf16[1,256,256]{2,1,0:T(8,128)(2,1)S(1)} %fusion.109), channel_id=1, source_target_pairs={{0,64},{64,0},{32,96},{96,32},{128,192},{192,128},{160,224},{224,1... | collective-permute-start | bytes 393224 | tf_op jit(solution)/shard_map/ppermute | solution.py:17
  394.7 27.3 %collective-permute-start.4 = (f32[4,256,1,256]{3,1,0,2:T(8,128)}, f32[4,256,1,256]{3,1,0,2:T(8,128)}, u32[]{:S(2)}, u32[]{:S(2)}) collective-permute-start(f32[4,256,1,256]{3,1,0,2:T(8,128)} %select_bitcast_fusion), channel_id=1, source_target_pairs={{0,128},{128,0},{32,160},{160,32},{64,192},{192,64},{96,224},{224,... | collective-permute-start | bytes 3145736 | tf_op jit(solution)/shard_map/ppermute | solution.py:17
  424.7 3.4 collective-permute-start.5
  428.2 27.1 %collective-permute-start.6 = (f32[256,256]{0,1:T(8,128)S(1)}, f32[256,256]{0,1:T(8,128)S(1)}, u32[]{:S(2)}, u32[]{:S(2)}) collective-permute-start(f32[256,256]{0,1:T(8,128)S(1)} %fusion.108), channel_id=1, source_target_pairs={{0,64},{64,0},{32,96},{96,32},{128,192},{192,128},{160,224},{224,1... | collective-permute-start | bytes 786440 | tf_op jit(solution)/shard_map/ppermute | solution.py:17
  455.3 10.2 %collective-permute-start.7 = (f32[256,256]{0,1:T(8,128)S(1)}, f32[256,256]{0,1:T(8,128)}, u32[]{:S(2)}, u32[]{:S(2)}) collective-permute-start(f32[256,256]{0,1:T(8,128)S(1)} %add.364), channel_id=1, source_target_pairs={{0,128},{128,0},{32,160},{160,32},{64,192},{192,64},{96,224},{224,... | collective-permute-start | bytes 786440 | tf_op jit(solution)/shard_map/ppermute | solution.py:17
  530.1 39.5 %copy-start.3 = (s32[2,32,256]{2,1,0:T(8,128)S(1)}, s32[2,32,256]{2,1,0:T(8,128)}, u32[]{:S(2)}) copy-start(s32[2,32,256]{2,1,0:T(8,128)} %param.18) | copy-start | bytes 196612
  530.1 143.1 %all-gather.18.cloned.1.call-start = ((), (), s32[]{:S(2)}) async-start(), calls=%async_computation.4 | async-start | bytes 4718592 | tf_op jit(solution)/shard_map/all_gather | solution.py:23
  569.5 304.9 %all-gather.14.cloned.1.call-start = ((), (), s32[]{:S(2)}) async-start(), calls=%async_computation.2 | async-start | bytes 1310720 | tf_op jit(solution)/shard_map/all_gather | solution.py:23
  673.3 5.0 copy-start.6
  676.3 3.2 collective-permute-start.8
  679.5 21.9 %collective-permute-start.9 = (bf16[1,256,256]{2,1,0:T(8,128)(2,1)S(1)}, bf16[1,256,256]{2,1,0:T(8,128)(2,1)S(1)}, u32[]{:S(2)}, u32[]{:S(2)}) collective-permute-start(bf16[1,256,256]{2,1,0:T(8,128)(2,1)S(1)} %fusion.107), channel_id=1, source_target_pairs={{0,64},{64,0},{32,96},{96,32},{128,192},{192,128},{160,224},{224,1... | collective-permute-start | bytes 393224 | tf_op jit(solution)/shard_map/ppermute | solution.py:17
  701.4 7.3 collective-permute-start.10
  709.2 3.8 copy-start.2
  710.5 16.7 %collective-permute-start.11 = (f32[2,256,1,256]{3,1,0,2:T(8,128)}, f32[2,256,1,256]{3,1,0,2:T(8,128)}, u32[]{:S(2)}, u32[]{:S(2)}) collective-permute-start(f32[2,256,1,256]{3,1,0,2:T(8,128)} %select_bitcast_fusion.1), channel_id=1, source_target_pairs={{0,256},{256,0},{32,288},{288,32},{64,320},{320,64},{96,352},{352,... | collective-permute-start | bytes 1572872 | tf_op jit(solution)/shard_map/ppermute | solution.py:17
  729.2 3.4 collective-permute-start.12
  732.6 27.4 %collective-permute-start.13 = (f32[256,256]{0,1:T(8,128)S(1)}, f32[256,256]{0,1:T(8,128)S(1)}, u32[]{:S(2)}, u32[]{:S(2)}) collective-permute-start(f32[256,256]{0,1:T(8,128)S(1)} %fusion.106), channel_id=1, source_target_pairs={{0,64},{64,0},{32,96},{96,32},{128,192},{192,128},{160,224},{224,1... | collective-permute-start | bytes 786440 | tf_op jit(solution)/shard_map/ppermute | solution.py:17
  760.1 10.1 %collective-permute-start.14 = (f32[256,256]{0,1:T(8,128)S(1)}, f32[256,256]{0,1:T(8,128)S(1)}, u32[]{:S(2)}, u32[]{:S(2)}) collective-permute-start(f32[256,256]{0,1:T(8,128)S(1)} %add.390), channel_id=1, source_target_pairs={{0,128},{128,0},{32,160},{160,32},{64,192},{192,64},{96,224},{224,... | collective-permute-start | bytes 786440 | tf_op jit(solution)/shard_map/ppermute | solution.py:17
  770.3 10.8 %collective-permute-start.15 = (f32[256,256]{0,1:T(8,128)S(1)}, f32[256,256]{0,1:T(8,128)S(1)}, u32[]{:S(2)}, u32[]{:S(2)}) collective-permute-start(f32[256,256]{0,1:T(8,128)S(1)} %add.391), channel_id=1, source_target_pairs={{0,256},{256,0},{32,288},{288,32},{64,320},{320,64},{96,352},{352,... | collective-permute-start | bytes 786440 | tf_op jit(solution)/shard_map/ppermute | solution.py:17
  843.6 104.0 %all-gather.20.cloned.1.call-start = ((), (), s32[]{:S(2)}) async-start(), calls=%async_computation.5 | async-start | bytes 2359296 | tf_op jit(solution)/shard_map/all_gather | solution.py:23
  949.7 3.2 collective-permute-start.16
  952.9 20.1 %collective-permute-start.17 = (bf16[1,256,256]{2,1,0:T(8,128)(2,1)S(1)}, bf16[1,256,256]{2,1,0:T(8,128)(2,1)S(1)}, u32[]{:S(2)}, u32[]{:S(2)}) collective-permute-start(bf16[1,256,256]{2,1,0:T(8,128)(2,1)S(1)} %fusion.105), channel_id=1, source_target_pairs={{0,64},{64,0},{32,96},{96,32},{128,192},{192,128},{160,224},{224,1... | collective-permute-start | bytes 393224 | tf_op jit(solution)/shard_map/ppermute | solution.py:17
  973.1 7.3 collective-permute-start.18
  980.4 8.4 collective-permute-start.19
Sparse Core Ops, SparseCore 0:
  99.6 73.0 all-gather.9
  177.1 182.3 all-gather.15
  530.2 36.2 all-gather.11
  569.6 103.6 all-gather.17
  843.7 30.6 all-gather.13
  876.9 70.6 all-gather.19
